TPU v7x, 512 devices: a whole 4x4x16 slice. The times are simulated.
512 devices in a mesh: tok: 32 (over z_hi, y, core), feat: 16 (over x, z_lo).
Axes of the slice: x: 4, y: 4, z: 16 (z_hi: 4, z_lo: 4; z = z_hi * 4 + z_lo), core: 2. Of those that a mesh axis runs over, the one named last changes fastest.
Arguments:
- calib: float32 [5120, 28672], P('tok', 'feat'), may hold values from -6 to 6
- weight: float32 [28672, 512], P('feat', 'tok'), may hold values from -0.03125 to 0.03125
Outputs:
- gram_product: float32 [512, 28672], P('tok', 'feat')
All inputs are finite; a program needn't handle non-finite values.
Results may differ from a plain program's by a relative error of at most 0.000098.
Values sent between devices are 32-bit elements; how exact they have to be, the bound alone decides.
A program may use at most 64 MiB of HBM per device.

v0:
```python
import math
import jax
import jax.numpy as jnp
from jax import lax
from jax.sharding import PartitionSpec as P


def shards(calib, weight):
    tokens_all = calib.shape[0] * lax.axis_size("tok")
    partial_rows = jnp.dot(
        calib,
        lax.all_gather(weight, "tok", axis=1, tiled=True),
        precision=lax.Precision.HIGHEST,
        preferred_element_type=jnp.float32,
    )
    mixed = lax.psum(partial_rows, "feat")
    factor = 1.0 / math.sqrt(tokens_all)
    term = lax.dot_general(
        mixed,
        calib,
        (((0,), (0,)), ((), ())),
        precision=lax.Precision.HIGHEST,
        preferred_element_type=jnp.float32,
    )
    return lax.psum_scatter(term * factor, "tok", scatter_dimension=0, tiled=True)


def solution(mesh):
    return jax.shard_map(
        shards,
        mesh=mesh,
        in_specs=(P("tok", "feat"), P("feat", "tok")),
        out_specs=P("tok", "feat"),
        check_vma=False,
    )
```

profile of v0, /device:TPU:4, one launch (start us, length us, event | category | flops | bytes accessed | tf_op | source)
XLA Modules:
  0.0 423.2 jit_solution(11789714599147911102)
XLA Ops:
  6.5 0.0 copy-start
  6.5 0.0 all-gather.2.cloned.1.call-start
  6.5 0.7 all-gather.2.cloned.1.call-update
  7.3 0.0 all-reduce.2.cloned.1.call-start
  7.3 98.3 %all-gather.2.cloned.1.call-done = f32[1792,512]{0,1:T(8,128)} async-done(((f32[1792,16]{0,1:T(8,128)}), f32[1792,512]{0,1:T(8,128)}) %all-gather.2.cloned.1.call-update) | async-done | bytes 3670032 | tf_op jit(solution)/shard_map/all_gather | solution.py:12
  105.6 0.0 copy-done
  105.6 6.6 %fusion = f32[160,512]{1,0:T(8,128)} fusion(f32[160,1792]{1,0:T(8,128)S(1)} %copy-done, f32[1792,512]{0,1:T(8,128)} %all-gather.2.cloned.1.call-done), kind=kOutput, calls=%fused_computation.1 | convolution fusion | flops 1761607680 | bytes 5144576 | tf_op jit(solution)/shard_map/dot_general | solution.py:10
  112.2 0.0 all-reduce.2.cloned.1.call-update
  112.2 0.0 reduce-scatter.2.cloned.1.call-start
  112.3 156.4 %all-reduce.2.cloned.1.call-done = f32[160,512]{1,0:T(8,128)} async-done(((f32[160,512]{1,0:T(8,128)}), f32[160,512]{1,0:T(8,128)}) %all-reduce.2.cloned.1.call-update) | async-done | bytes 327696 | tf_op jit(solution)/shard_map/psum | solution.py:16
  268.7 5.9 %convolution_multiply_fusion = f32[512,1792]{1,0:T(8,128)} fusion(f32[160,512]{1,0:T(8,128)} %all-reduce.2.cloned.1.call-done, f32[160,1792]{1,0:T(8,128)S(1)} %copy-done), kind=kOutput, calls=%fused_computation | convolution fusion | flops 1762525184 | bytes 5144576 | tf_op jit(solution)/shard_map/dot_general | solution.py:18
  274.6 0.0 reduce-scatter.2.cloned.1.call-update
  274.6 142.1 %reduce-scatter.2.cloned.1.call-done = f32[16,1792]{1,0:T(8,128)} async-done(((f32[512,1792]{1,0:T(8,128)}), f32[16,1792]{1,0:T(8,128)}) %reduce-scatter.2.cloned.1.call-update) | async-done | bytes 114704 | tf_op jit(solution)/shard_map/reduce_scatter | solution.py:25
Async XLA Ops:
  6.5 99.1 %copy-start = (f32[160,1792]{1,0:T(8,128)S(1)}, f32[160,1792]{1,0:T(8,128)}, u32[]{:S(2)}) copy-start(f32[160,1792]{1,0:T(8,128)} %param.2) | copy-start | bytes 3440644
  6.5 99.1 %all-gather.2.cloned.1.call-start = ((), (), s32[]{:S(2)}) async-start(), calls=%async_computation.1 | async-start | bytes 3784704 | tf_op jit(solution)/shard_map/all_gather | solution.py:12
  7.3 261.4 %all-reduce.2.cloned.1.call-start = ((), (), s32[]{:S(2)}) async-start(), calls=%async_computation.2 | async-start | bytes 655360 | tf_op jit(solution)/shard_map/psum | solution.py:16
  112.2 304.5 %reduce-scatter.2.cloned.1.call-start = ((), (), s32[]{:S(2)}) async-start(), calls=%async_computation.3 | async-start | bytes 3784704 | tf_op jit(solution)/shard_map/reduce_scatter | solution.py:25
Sparse Core Ops, SparseCore 0:
  10.5 95.1 all-gather.1
  112.3 156.3 all-reduce.1
  274.7 141.9 reduce-scatter.1
where the time goes:
time: 423 us
  waiting for transfers between devices  398 us (94%)
  between operations  13.1 us (3%)
  matrix products  12.4 us (3%)
    psum x1, waiting for transfers between devices, shards(): mixed = lax.psum(partial_rows, 'feat')  156 us
    reduce_scatter x1, waiting for transfers between devices, shards(): lax.psum_scatter(term * factor, 'tok', scatter_dimension=0, tiled=True)  142 us
    all_gather x1, waiting for transfers between devices, shards(): lax.all_gather(weight, 'tok', axis=1, tiled=True)  98.3 us
  transfers between devices with their start and end apart: 3, of which 3 were waited for; matrix products, arithmetic and copies ran while one was open for 0% of the time, Pallas kernels for 0%

commit v1 on v0

--- a/solution.py
+++ b/solution.py
@@ -9,7 +9,9 @@
     tokens_all = calib.shape[0] * lax.axis_size("tok")
     partial_rows = jnp.dot(
         calib,
-        lax.all_gather(weight, "tok", axis=1, tiled=True),
+        jnp.concatenate(
+            lax.all_to_all(jnp.stack([weight] * lax.axis_size("tok")), "tok", 0, 0), axis=1
+        ),
         precision=lax.Precision.HIGHEST,
         preferred_element_type=jnp.float32,
     )

time: 423 us -> 507 us (1.20)
  blocking collectives: 0 us -> 183 us
  waiting for transfers between devices: 398 us -> 298 us
    all_to_all x0 -> x1, blocking collectives: none -> 183 us  [shards(): lax.all_to_all(jnp.stack([weight] * lax.axis_size('tok')), 'tok', 0, 0)]
    all_gather x1 -> x0, waiting for transfers between devices: 98.3 us -> none  [shards(): lax.all_gather(weight, 'tok', axis=1, tiled=True)]
  transfers between devices with their start and end apart: 3 -> 2, of which waited for: 3 -> 2; matrix products, arithmetic and copies ran while one was open for 0% -> 0% of each run, Pallas kernels for 0% -> 0%
where the time goes in v1:
time: 507 us
  waiting for transfers between devices  298 us (59%)
  blocking collectives  183 us (36%)
  between operations  13.4 us (3%)
  matrix products  10.4 us (2%)
    all_to_all x1, blocking collectives, shards(): lax.all_to_all(jnp.stack([weight] * lax.axis_size('tok')), 'tok', 0, 0)  183 us
    psum x1, waiting for transfers between devices, shards(): mixed = lax.psum(partial_rows, 'feat')  156 us
    reduce_scatter x1, waiting for transfers between devices, shards(): lax.psum_scatter(term * factor, 'tok', scatter_dimension=0, tiled=True)  142 us
  transfers between devices with their start and end apart: 2, of which 2 were waited for; matrix products, arithmetic and copies ran while one was open for 0% of the time, Pallas kernels for 0%

profile of v1, /device:TPU:4, one launch (start us, length us, event | category | flops | bytes accessed | tf_op | source)
XLA Modules:
  0.0 506.9 jit_solution(18007573054753200745)
XLA Ops:
  6.5 0.0 copy-start
  6.5 0.0 all-reduce.2.cloned.1.call-start
  6.5 1.4 stack.2
  7.9 183.4 %all_to_all.5 = f32[32,1792,16]{1,2,0:T(8,128)S(1)} all-to-all(f32[32,1792,16]{1,2,0:T(8,128)S(1)} %stack.2), channel_id=1, replica_groups=mesh['tok'=32,'feat'=16] {'tok'}, dimensions={0} | all-to-all | bytes 7340032 | tf_op jit(solution)/shard_map/all_to_all | solution.py:13
  191.4 0.0 copy-done
  191.4 4.5 fusion
  195.9 0.0 all-reduce.2.cloned.1.call-update
  196.0 0.0 reduce-scatter.2.cloned.1.call-start
  196.0 156.4 %all-reduce.2.cloned.1.call-done = f32[160,512]{1,0:T(8,128)} async-done(((f32[160,512]{1,0:T(8,128)}), f32[160,512]{1,0:T(8,128)}) %all-reduce.2.cloned.1.call-update) | async-done | bytes 327696 | tf_op jit(solution)/shard_map/psum | solution.py:18
  352.4 5.9 %convolution_multiply_fusion = f32[512,1792]{1,0:T(8,128)} fusion(f32[160,512]{1,0:T(8,128)} %all-reduce.2.cloned.1.call-done, f32[160,1792]{1,0:T(8,128)S(1)} %copy-done), kind=kOutput, calls=%fused_computation | convolution fusion | flops 1762525184 | bytes 5144576 | tf_op jit(solution)/shard_map/dot_general | solution.py:20
  358.3 0.0 reduce-scatter.2.cloned.1.call-update
  358.3 141.8 %reduce-scatter.2.cloned.1.call-done = f32[16,1792]{1,0:T(8,128)} async-done(((f32[512,1792]{1,0:T(8,128)}), f32[16,1792]{1,0:T(8,128)}) %reduce-scatter.2.cloned.1.call-update) | async-done | bytes 114704 | tf_op jit(solution)/shard_map/reduce_scatter | solution.py:27
Async XLA Ops:
  6.5 184.9 %copy-start = (f32[160,1792]{1,0:T(8,128)S(1)}, f32[160,1792]{1,0:T(8,128)}, u32[]{:S(2)}) copy-start(f32[160,1792]{1,0:T(8,128)} %param.2) | copy-start | bytes 3440644
  6.5 345.9 %all-reduce.2.cloned.1.call-start = ((), (), s32[]{:S(2)}) async-start(), calls=%async_computation.2 | async-start | bytes 655360 | tf_op jit(solution)/shard_map/psum | solution.py:18
  196.0 304.1 %reduce-scatter.2.cloned.1.call-start = ((), (), s32[]{:S(2)}) async-start(), calls=%async_computation.3 | async-start | bytes 3784704 | tf_op jit(solution)/shard_map/reduce_scatter | solution.py:27
Sparse Core Ops, SparseCore 0:
  196.1 156.2 all-reduce.1
  358.4 141.6 reduce-scatter.1

commit v2 on v0

--- a/solution.py
+++ b/solution.py
@@ -13,7 +13,7 @@
         precision=lax.Precision.HIGHEST,
         preferred_element_type=jnp.float32,
     )
-    mixed = lax.psum(partial_rows, "feat")
+    mixed = jnp.sum(lax.all_gather(partial_rows, "feat"), axis=0)
     factor = 1.0 / math.sqrt(tokens_all)
     term = lax.dot_general(
         mixed,

time: 423 us -> 385 us (0.910)
  the two profiles are of different devices: /device:TPU:4 before, /device:TPU:6 now
where the time goes in v2:
time: 385 us
  waiting for transfers between devices  357 us (93%)
  between operations  13.1 us (3%)
  matrix products  11.5 us (3%)
    reduce_scatter x1, waiting for transfers between devices, shards(): lax.psum_scatter(term * factor, 'tok', scatter_dimension=0, tiled=True)  137 us
    all_gather x1, waiting for transfers between devices, shards(): mixed = jnp.sum(lax.all_gather(partial_rows, 'feat'), axis=0)  121 us
    all_gather x1, waiting for transfers between devices, shards(): lax.all_gather(weight, 'tok', axis=1, tiled=True)  98.3 us
  transfers between devices with their start and end apart: 3, of which 3 were waited for; matrix products, arithmetic and copies ran while one was open for 0% of the time, Pallas kernels for 0%

profile of v2, /device:TPU:6, one launch (start us, length us, event | category | flops | bytes accessed | tf_op | source)
XLA Modules:
  0.0 384.6 jit_solution(3173620687626841803)
XLA Ops:
  6.5 0.0 copy-start
  6.5 0.0 all-gather.4.cloned.1.call-start
  6.5 0.7 all-gather.4.cloned.1.call-update
  7.3 0.0 all-gather.6.cloned.1.call-start
  7.3 98.3 %all-gather.4.cloned.1.call-done = f32[1792,512]{0,1:T(8,128)} async-done(((f32[1792,16]{0,1:T(8,128)}), f32[1792,512]{0,1:T(8,128)}) %all-gather.4.cloned.1.call-update) | async-done | bytes 3670032 | tf_op jit(solution)/shard_map/all_gather | solution.py:12
  105.6 0.0 copy-done
  105.6 6.6 %fusion = f32[160,512]{1,0:T(8,128)} fusion(f32[160,1792]{1,0:T(8,128)S(1)} %copy-done, f32[1792,512]{0,1:T(8,128)} %all-gather.4.cloned.1.call-done), kind=kOutput, calls=%fused_computation.1 | convolution fusion | flops 1761607680 | bytes 5144576 | tf_op jit(solution)/shard_map/dot_general | solution.py:10
  112.2 0.0 all-gather.6.cloned.1.call-update
  112.2 0.0 reduce-scatter.2.cloned.1.call-start
  112.3 120.7 %all-gather.6.cloned.1.call-done = f32[2560,512]{1,0:T(8,128)} async-done(((f32[160,512]{1,0:T(8,128)}), f32[2560,512]{1,0:T(8,128)}) %all-gather.6.cloned.1.call-update) | async-done | bytes 5242896 | tf_op jit(solution)/shard_map/all_gather | solution.py:16
  233.0 3.1 reduce_sum.9
  236.1 4.9 %convolution_multiply_fusion = f32[512,1792]{1,0:T(8,128)} fusion(f32[160,512]{1,0:T(8,128)S(1)} %reduce_sum.9, f32[160,1792]{1,0:T(8,128)S(1)} %copy-done), kind=kOutput, calls=%fused_computation | convolution fusion | flops 1762525184 | bytes 5144576 | tf_op jit(solution)/shard_map/dot_general | solution.py:18
  241.0 0.0 reduce-scatter.2.cloned.1.call-update
  241.0 137.1 %reduce-scatter.2.cloned.1.call-done = f32[16,1792]{1,0:T(8,128)} async-done(((f32[512,1792]{1,0:T(8,128)}), f32[16,1792]{1,0:T(8,128)}) %reduce-scatter.2.cloned.1.call-update) | async-done | bytes 114704 | tf_op jit(solution)/shard_map/reduce_scatter | solution.py:25
Async XLA Ops:
  6.5 99.1 %copy-start = (f32[160,1792]{1,0:T(8,128)S(1)}, f32[160,1792]{1,0:T(8,128)}, u32[]{:S(2)}) copy-start(f32[160,1792]{1,0:T(8,128)} %param.2) | copy-start | bytes 3440644
  6.5 99.0 %all-gather.4.cloned.1.call-start = ((), (), s32[]{:S(2)}) async-start(), calls=%async_computation.1 | async-start | bytes 3784704 | tf_op jit(solution)/shard_map/all_gather | solution.py:12
  7.3 225.7 %all-gather.6.cloned.1.call-start = ((), (), s32[]{:S(2)}) async-start(), calls=%async_computation.3 | async-start | bytes 5570560 | tf_op jit(solution)/shard_map/all_gather | solution.py:16
  112.2 265.8 %reduce-scatter.2.cloned.1.call-start = ((), (), s32[]{:S(2)}) async-start(), calls=%async_computation.2 | async-start | bytes 3784704 | tf_op jit(solution)/shard_map/reduce_scatter | solution.py:25
Sparse Core Ops, SparseCore 0:
  10.5 95.0 all-gather.3
  112.3 120.6 all-gather.5
  241.1 136.8 reduce-scatter.1
